TPU v7x, 512 devices: a whole 4x8x8 slice. The times are simulated.
512 devices in a mesh: ent: 128 (over y, z, core), rep: 4 (over x).
Axes of the slice: x: 4, y: 8, z: 8, core: 2. Of those that a mesh axis runs over, the one named last changes fastest.
Arguments:
- entity_table: float32 [65536, 200], P('ent'), may hold values from -6 to 6
- relation_table: bfloat16 [822, 200], replicated, may hold values from -12 to 12
- filters: float32 [32, 9], replicated, may hold values from -2 to 2
- projection: bfloat16 [9728, 200], replicated, may hold values from -0.0625 to 0.0625
- request_owner: int32 [163840, 1], P(('ent', 'rep')), may hold values from 0 to 127; in each aligned block of 320 rows (0 to 319, 320 to 639, ...) at most 4 rows name the same one
- request_row: int32 [163840], P(('ent', 'rep')), may hold values from 0 to 511
- relation_id: int32 [65536], P(('ent', 'rep')), may hold values from 0 to 821
- rare_flag: int32 [65536], P('ent'), may hold values 0 or 1
- running_norm: float32 [], replicated, may hold values from 2 to 6
Outputs:
- new_table: float32 [65536, 200], P('ent')
- filter_grad: float32 [32, 9], replicated
Inputs may be any that keep to these rules, and one draw needn't show every extreme that they name: `request_owner`: among the requests of one device no owner shard is named more than 4 times, a bound that some block reaches.
All inputs are finite; a program needn't handle non-finite values. No bound on the sum of `rare_flag` on one device may be relied on, other than what follows from the above.
Results may differ from a plain program's by a relative error of at most 0.002.
Values sent between devices are 32-bit elements; how exact they have to be, the bound alone decides.
A program may use at most 64 MiB of HBM per device.

v0:
```python
import jax
import jax.numpy as jnp
from jax import lax
from jax.sharding import PartitionSpec as P

D = 200
ROWS = 20
learn_rate = 0.5
norm_eps = 1e-06


def conv_act(head_rows, rel_rows, filters):
    count = head_rows.shape[0]
    stacked = jnp.concatenate(
        [head_rows.reshape(count, ROWS, D // ROWS), rel_rows.reshape(count, ROWS, D // ROWS)],
        axis=1,
    )[:, None]
    kernel = filters.reshape(filters.shape[0], 1, 3, 3)
    conv_out = lax.conv_general_dilated(
        stacked, kernel, (1, 1), "VALID", precision=lax.Precision.HIGHEST
    )
    return jax.nn.silu(conv_out).reshape(count, -1)


def block_step(row_values, rel_rows, filters, projection, batch_rows, neg_count):
    head_rows = row_values[:batch_rows]
    pos_rows = row_values[batch_rows : 2 * batch_rows]
    neg_rows = row_values[2 * batch_rows :]
    activated, pullback = jax.vjp(
        lambda head_part, filt_part: conv_act(head_part, rel_rows, filt_part), head_rows, filters
    )
    features = activated.astype(jnp.bfloat16)
    projected = jnp.dot(features, projection, preferred_element_type=jnp.float32)
    sig_proj = jax.nn.sigmoid(projected)
    hidden = projected * sig_proj
    score_pos = jnp.sum(hidden * pos_rows, 1)
    score_neg = jnp.dot(hidden, neg_rows.T, precision=lax.Precision.HIGHEST)
    grad_pos = -jax.nn.sigmoid(-score_pos)
    grad_neg = jax.nn.sigmoid(score_neg) / neg_count
    pos_grad_rows = grad_pos[:, None] * hidden
    neg_grad_rows = jnp.dot(grad_neg.T, hidden, precision=lax.Precision.HIGHEST)
    grad_hidden = grad_pos[:, None] * pos_rows + jnp.dot(
        grad_neg, neg_rows, precision=lax.Precision.HIGHEST
    )
    grad_proj = (grad_hidden * sig_proj * (1.0 + projected * (1.0 - sig_proj))).astype(jnp.bfloat16)
    grad_feat = lax.dot_general(
        grad_proj, projection, (((1,), (1,)), ((), ())), preferred_element_type=jnp.float32
    )
    head_grad_rows, filter_part = pullback(grad_feat)
    return (jnp.concatenate([head_grad_rows, pos_grad_rows, neg_grad_rows], axis=0), filter_part)


def body(
    entity_table,
    relation_table,
    filters,
    projection,
    request_owner,
    request_row,
    relation_id,
    rare_flag,
    running_norm,
):
    ent_count = lax.axis_size("ent")
    rep_count = lax.axis_size("rep")
    req_count = request_row.shape[0]
    batch_rows = relation_id.shape[0]
    neg_count = req_count - 2 * batch_rows
    width = entity_table.shape[1]
    slots_each = max(2, 3 * req_count // (2 * ent_count) + 1)
    owner_shard = request_owner[:, 0]
    onehot = (owner_shard[:, None] == jnp.arange(ent_count, dtype=jnp.int32)[None, :]).astype(
        jnp.int32
    )
    slot_index = jnp.sum(jnp.cumsum(onehot, 0) * onehot, 1) - 1
    slot_place = owner_shard * slots_each + slot_index
    send_ids = (
        jnp.zeros((ent_count * slots_each,), jnp.int32)
        .at[slot_place]
        .set(request_row)
        .reshape(ent_count, slots_each)
    )
    wanted = lax.all_to_all(send_ids, "ent", split_axis=0, concat_axis=0, tiled=True)
    found_rows = entity_table[wanted]
    fetched = lax.all_to_all(found_rows, "ent", split_axis=0, concat_axis=0, tiled=True)
    row_values = fetched.reshape(-1, width)[slot_place]
    rel_rows = relation_table[relation_id].astype(jnp.float32)
    grads, filter_part = block_step(
        row_values, rel_rows, filters, projection, batch_rows, neg_count
    )
    send_grads = (
        jnp.zeros((ent_count * slots_each, width), jnp.float32)
        .at[slot_place]
        .set(grads)
        .reshape(ent_count, slots_each, width)
    )
    received = lax.all_to_all(send_grads, "ent", split_axis=0, concat_axis=0, tiled=True)
    all_ids = lax.all_gather(wanted, "rep", axis=0, tiled=True)
    all_grads = lax.all_gather(received, "rep", axis=0, tiled=True)
    summed_grad = (
        jnp.zeros(entity_table.shape, jnp.float32)
        .at[all_ids.reshape(-1)]
        .add(all_grads.reshape(-1, width))
    )
    updated = entity_table - learn_rate * summed_grad
    row_norms = jnp.sqrt(jnp.sum(updated * updated, 1) + norm_eps)
    local_norm = jnp.sum(row_norms)
    filter_total = lax.psum(filter_part, ("ent", "rep"))
    norm_total = lax.psum(local_norm, "ent")
    filter_grad = filter_total / (batch_rows * ent_count * rep_count)
    target = 0.25 * running_norm + 0.75 * norm_total / (entity_table.shape[0] * ent_count)
    new_table = jnp.where(
        (rare_flag == 1)[:, None], updated * (target / row_norms)[:, None], updated
    )
    return (new_table, filter_grad)


def solution(mesh):
    in_specs = (
        P("ent", None),
        P(),
        P(),
        P(),
        P(("ent", "rep"), None),
        P(("ent", "rep")),
        P(("ent", "rep")),
        P("ent"),
        P(),
    )
    out_specs = (P("ent", None), P())
    return jax.shard_map(body, mesh=mesh, in_specs=in_specs, out_specs=out_specs, check_vma=False)
```

profile of v0, /device:TPU:1, one launch (start us, length us, event | category | flops | bytes accessed | tf_op | source)
XLA Modules:
  0.0 538.2 jit_solution(8350565503353187962)
XLA Ops:
  9.2 3.1 scatter_custom_fusion
  13.1 18.4 %all-to-all-start = ((s32[128,1,4]{2,1,0:T(1,128)}), s32[128,1,4]{2,1,0:T(1,128)S(1)}, u32[]{:S(2)}, u32[]{:S(2)}) async-start(s32[128,1,4]{2,1,0:T(1,128)} %bitcast.4), calls=%async_computation | async-start | bytes 131072 | tf_op jit(solution)/shard_map/all_to_all | solution.py:83
  31.5 1.2 copy.117
  32.7 10.2 %all-to-all-done = s32[128,1,4]{2,1,0:T(1,128)S(1)} async-done(((s32[128,1,4]{2,1,0:T(1,128)}), s32[128,1,4]{2,1,0:T(1,128)S(1)}, u32[]{:S(2)}, u32[]{:S(2)}) %all-to-all-start) | async-done | bytes 2080 | tf_op jit(solution)/shard_map/all_to_all | solution.py:83
  43.6 1.6 gather_fusion
  46.1 5.7 %all-to-all-start.1 = ((f32[128,4,200]{2,1,0:T(4,128)}), f32[128,4,200]{2,1,0:T(4,128)S(1)}, u32[]{:S(2)}, u32[]{:S(2)}) async-start(f32[128,4,200]{2,1,0:T(4,128)} %reshape.144), calls=%async_computation.1 | async-start | bytes 1048576 | tf_op jit(solution)/shard_map/all_to_all | solution.py:85
  53.6 17.8 %all-to-all-done.1 = f32[128,4,200]{2,1,0:T(4,128)S(1)} async-done(((f32[128,4,200]{2,1,0:T(4,128)}), f32[128,4,200]{2,1,0:T(4,128)S(1)}, u32[]{:S(2)}, u32[]{:S(2)}) %all-to-all-start.1) | async-done | bytes 409632 | tf_op jit(solution)/shard_map/all_to_all | solution.py:85
  71.6 1.6 gather_fusion.1
  74.1 7.1 %multiply_convert_fusion = (bf16[128,32,38,8]{0,1,3,2:T(8,128)(2,1)S(1)}, f32[128,32,38,8]{0,1,3,2:T(8,128)}) fusion(f32[32,1,3,3]{0,1,3,2:T(1,128)S(1)} %reshape.195, f32[128,1,40,10]{0,2,3,1:T(8,128)S(1)} %bitcast.46), kind=kOutput, calls=%fused_computation.9 | convolution fusion | flops 140705792 | bytes 7677056 | tf_op jit(solution)/shard_map/jvp()/conv_general_dilated | solution.py:19
  82.1 1.6 copy.123
  83.8 3.5 multiply_reduce_fusion.1
  88.3 2.0 fusion.30
  90.4 2.6 fusion.1
  93.1 2.2 copy-done
  95.3 23.1 %fusion.29 = f32[128,1,40,10]{0,1,3,2:T(1,128)S(1)} fusion(f32[128,32,38,8]{0,1,3,2:T(8,128)S(1)} %fusion.1, f32[32,1,3,3]{0,1,3,2:T(1,128)S(1)} %reshape.195), kind=kOutput, calls=%fused_computation.68 | convolution fusion | flops 134479872 | bytes 5186688 | tf_op jit(solution)/shard_map/transpose(jvp())/conv_general_dilated | solution.py:19
  118.7 1.9 scatter_custom_fusion.1
  120.7 26.3 %all_to_all.25 = f32[128,4,200]{2,1,0:T(4,128)S(1)} all-to-all(f32[128,4,200]{2,1,0:T(4,128)S(1)} %reshape.138), channel_id=1, replica_groups=mesh['ent'=128,'rep'=4] {'ent'}, dimensions={0} | all-to-all | bytes 819200 | tf_op jit(solution)/shard_map/all_to_all | solution.py:97
  148.7 8.4 %all-gather = s32[512,1,4]{0,2,1:T(4,128)S(1)} all-gather(s32[128,1,4]{0,2,1:T(4,128)S(1)} %copy.96), channel_id=2, replica_groups=mesh['ent'=128,'rep'=4] {'rep'}, dimensions={0}, use_global_device_ids=true | all-gather | bytes 10240 | tf_op jit(solution)/shard_map/all_gather | solution.py:98
  157.5 9.4 %convolution_reduce_fusion = f32[32,3,3]{0,2,1:T(4,128)S(1)} fusion(f32[128,32,38,8]{0,1,3,2:T(8,128)} %copy-done, f32[128,1,40,10]{0,2,3,1:T(8,128)S(1)} %bitcast.47), kind=kOutput, calls=%fused_computation.20 | convolution fusion | flops 134479872 | bytes 5186688 | tf_op jit(solution)/shard_map/transpose(jvp())/conv_general_dilated | solution.py:19
  166.9 97.7 %psum.15 = f32[32,9]{0,1:T(8,128)S(1)} all-reduce(f32[32,9]{0,1:T(8,128)S(1)} %reshape.140), channel_id=1, replica_groups=mesh['ent'=128,'rep'=4] {'ent','rep'}, use_global_device_ids=true, to_apply=%region_10.11 | all-reduce | flops 288 | bytes 2304 | tf_op jit(solution)/shard_map/psum | solution.py:108
  264.6 2.0 copy.116
  266.6 1.8 reshape.187
  268.3 12.1 %scatter_custom_fusion.2 = f32[512,200]{1,0:T(8,128)S(1)} fusion(s32[2048]{0:T(1024)S(1)} %bitcast.53, f32[2048,200]{1,0:T(8,128)} %reshape.187, f32[]{:T(128)} %constant.16.clone.1), kind=kCustom, calls=%fused_computation.28 | custom fusion | flops 409600 | bytes 410112 | tf_op jit(solution)/shard_map/scatter-add | solution.py:103
  281.8 247.5 %psum.14 = f32[]{:T(128)} all-reduce(f32[]{:T(128)} %sqrt_reduce_fusion), channel_id=1, replica_groups=mesh['ent'=128,'rep'=4] {'ent'}, use_global_device_ids=true, to_apply=%region_9.10 | all-reduce | flops 1 | bytes 8 | tf_op jit(solution)/shard_map/psum | solution.py:109
  (83 shorter events, 13.4 us)
Async XLA Ops:
  8.0 44.3 %copy-start.5 = (bf16[822,200]{0,1:T(8,128)(2,1)S(1)}, bf16[822,200]{0,1:T(8,128)(2,1)}, u32[]{:S(2)}) copy-start(bf16[822,200]{0,1:T(8,128)(2,1)} %param.10) | copy-start | bytes 986404
  8.2 44.3 %copy-start.9 = (s32[128]{0:T(128)S(1)}, s32[128]{0:T(128)}, u32[]{:S(2)}) copy-start(s32[128]{0:T(128)} %param.15) | copy-start | bytes 1540
  8.5 45.1 %copy-start.6 = (f32[32,9]{0,1:T(8,128)S(1)}, f32[32,9]{0,1:T(8,128)}, u32[]{:S(2)}) copy-start(f32[32,9]{0,1:T(8,128)} %param.11) | copy-start | bytes 3460
  9.2 62.3 %copy-start.7 = (s32[320]{0:T(512)}, s32[320]{0:T(512)S(1)}, u32[]{:S(2)}) copy-start(s32[320]{0:T(512)S(1)} %fusion.22) | copy-start | bytes 3844
  13.1 29.9 %all-to-all-start = ((s32[128,1,4]{2,1,0:T(1,128)}), s32[128,1,4]{2,1,0:T(1,128)S(1)}, u32[]{:S(2)}, u32[]{:S(2)}) async-start(s32[128,1,4]{2,1,0:T(1,128)} %bitcast.4), calls=%async_computation | async-start | bytes 131072 | tf_op jit(solution)/shard_map/all_to_all | solution.py:83
  42.9 0.6 copy-start.2
  46.1 25.3 %all-to-all-start.1 = ((f32[128,4,200]{2,1,0:T(4,128)}), f32[128,4,200]{2,1,0:T(4,128)S(1)}, u32[]{:S(2)}, u32[]{:S(2)}) async-start(f32[128,4,200]{2,1,0:T(4,128)} %reshape.144), calls=%async_computation.1 | async-start | bytes 1048576 | tf_op jit(solution)/shard_map/all_to_all | solution.py:85
  51.8 212.8 %all-gather.3.cloned.1.call-start = ((), (), s32[]{:S(2)}) async-start(), calls=%async_computation.3 | async-start | bytes 2048000 | tf_op jit(solution)/shard_map/all_gather | solution.py:99
  83.8 4.1 copy-start.4
  83.8 4.5 copy-start.1
  87.5 2.8 slice-start
  88.3 2.1 slice-start.1
  93.1 2.2 copy-start
  95.3 53.4 %copy-start.8 = (s32[512]{0:T(512)S(1)}, s32[512]{0:T(512)}, u32[]{:S(2)}) copy-start(s32[512]{0:T(512)} %param.16) | copy-start | bytes 6148
  95.3 53.4 %copy-start.3 = (s32[128,1,4]{2,1,0:T(1,128)S(1)}, s32[128,1,4]{2,1,0:T(1,128)}, u32[]{:S(2)}) copy-start(s32[128,1,4]{2,1,0:T(1,128)} %copy-done.2) | copy-start | bytes 6148
Sparse Core Ops, SparseCore 0:
  148.1 28.8 all-gather.2
where the time goes:
time: 544 us; the launch traced here: 538 us
  blocking collectives  380 us (70%)
  matrix products  46 us (8%)
  waiting for transfers between devices  28 us (5%)
  local copies, waits for them, and re-layouts  25.1 us (5%)
  starting transfers between devices  24.6 us (5%)
  other arithmetic  18.4 us (3%)
  between operations  16.1 us (3%)
    psum x1, blocking collectives, body(): norm_total = lax.psum(local_norm, 'ent')  247 us
    psum x1, blocking collectives, body(): filter_total = lax.psum(filter_part, ('ent', 'rep'))  97.7 us
    conv_general_dilated x3, matrix products, conv_act(): lax.conv_general_dilated(stacked, kernel, (1, 1), 'VALID', precision=lax....  39.5 us
    all_to_all x1, blocking collectives, body(): lax.all_to_all(send_grads, 'ent', split_axis=0, concat_axis=0, tiled=True)  26.3 us
    all_to_all x1, starting transfers between devices, body(): lax.all_to_all(send_ids, 'ent', split_axis=0, concat_axis=0, tiled=True)  18.4 us
    all_to_all x1, waiting for transfers between devices, body(): lax.all_to_all(found_rows, 'ent', split_axis=0, concat_axis=0, tiled=True)  17.8 us
    scatter-add x1, other arithmetic, body(): summed_grad = jnp.zeros(entity_table.shape, jnp.float32).at[all_ids.resha...  12.1 us
  transfers between devices with their start and end apart: 3, of which 2 were waited for; matrix products, arithmetic and copies ran while one was open for 2% of the time, Pallas kernels for 0%

commit v1 on v0

--- a/solution.py
+++ b/solution.py
@@ -105,7 +105,8 @@
     updated = entity_table - learn_rate * summed_grad
     row_norms = jnp.sqrt(jnp.sum(updated * updated, 1) + norm_eps)
     local_norm = jnp.sum(row_norms)
-    filter_total = lax.psum(filter_part, ("ent", "rep"))
+    search_words_over_axis = lambda original: lax.psum(lax.psum(original, "ent"), "rep")
+    filter_total = search_words_over_axis(filter_part)
     norm_total = lax.psum(local_norm, "ent")
     filter_grad = filter_total / (batch_rows * ent_count * rep_count)
     target = 0.25 * running_norm + 0.75 * norm_total / (entity_table.shape[0] * ent_count)

time: 544 us -> 477 us (0.88)
  blocking collectives: 380 us -> 300 us
  waiting for transfers between devices: 28 us -> 38.1 us
    psum x1, blocking collectives: 97.7 us -> 7.85 us  [body(): lax.psum(lax.psum(original, 'ent'), 'rep')]
    all_gather x1, waiting for transfers between devices: 0.01 us -> 10.1 us  [body(): all_grads = lax.all_gather(received, 'rep', axis=0, tiled=True)]
    psum x1, blocking collectives: 247 us -> 257 us  [body(): norm_total = lax.psum(local_norm, 'ent')]
  transfers between devices with their start and end apart: 3 -> 3, of which waited for: 2 -> 3; matrix products, arithmetic and copies ran while one was open for 2% -> 3% of each run, Pallas kernels for 0% -> 0%
where the time goes in v1:
time: 477 us; the launch traced here: 468 us
  blocking collectives  300 us (63%)
  matrix products  46 us (10%)
  waiting for transfers between devices  38.1 us (8%)
  local copies, waits for them, and re-layouts  25.1 us (5%)
  starting transfers between devices  24.6 us (5%)
  other arithmetic  18.4 us (4%)
  between operations  16.1 us (3%)
    psum x1, blocking collectives, body(): norm_total = lax.psum(local_norm, 'ent')  257 us
    conv_general_dilated x3, matrix products, conv_act(): lax.conv_general_dilated(stacked, kernel, (1, 1), 'VALID', precision=lax....  39.5 us
    all_to_all x1, blocking collectives, body(): lax.all_to_all(send_grads, 'ent', split_axis=0, concat_axis=0, tiled=True)  26.3 us
    all_to_all x1, starting transfers between devices, body(): lax.all_to_all(send_ids, 'ent', split_axis=0, concat_axis=0, tiled=True)  18.4 us
    all_to_all x1, waiting for transfers between devices, body(): lax.all_to_all(found_rows, 'ent', split_axis=0, concat_axis=0, tiled=True)  17.8 us
    scatter-add x1, other arithmetic, body(): summed_grad = jnp.zeros(entity_table.shape, jnp.float32).at[all_ids.resha...  12.1 us
    all_to_all x1, waiting for transfers between devices, body(): lax.all_to_all(send_ids, 'ent', split_axis=0, concat_axis=0, tiled=True)  10.2 us
    all_gather x1, waiting for transfers between devices, body(): all_grads = lax.all_gather(received, 'rep', axis=0, tiled=True)  10.1 us
  transfers between devices with their start and end apart: 3, of which 3 were waited for; matrix products, arithmetic and copies ran while one was open for 3% of the time, Pallas kernels for 0%

profile of v1, /device:TPU:1, one launch (start us, length us, event | category | flops | bytes accessed | tf_op | source)
XLA Modules:
  0.0 468.3 jit_solution(6184904011701899252)
XLA Ops:
  9.2 3.1 scatter_custom_fusion
  13.1 18.4 %all-to-all-start = ((s32[128,1,4]{2,1,0:T(1,128)}), s32[128,1,4]{2,1,0:T(1,128)S(1)}, u32[]{:S(2)}, u32[]{:S(2)}) async-start(s32[128,1,4]{2,1,0:T(1,128)} %bitcast.4), calls=%async_computation | async-start | bytes 131072 | tf_op jit(solution)/shard_map/all_to_all | solution.py:83
  32.7 10.2 %all-to-all-done = s32[128,1,4]{2,1,0:T(1,128)S(1)} async-done(((s32[128,1,4]{2,1,0:T(1,128)}), s32[128,1,4]{2,1,0:T(1,128)S(1)}, u32[]{:S(2)}, u32[]{:S(2)}) %all-to-all-start) | async-done | bytes 2080 | tf_op jit(solution)/shard_map/all_to_all | solution.py:83
  43.6 1.6 gather_fusion
  46.1 5.7 %all-to-all-start.1 = ((f32[128,4,200]{2,1,0:T(4,128)}), f32[128,4,200]{2,1,0:T(4,128)S(1)}, u32[]{:S(2)}, u32[]{:S(2)}) async-start(f32[128,4,200]{2,1,0:T(4,128)} %reshape.144), calls=%async_computation.1 | async-start | bytes 1048576 | tf_op jit(solution)/shard_map/all_to_all | solution.py:85
  53.6 17.8 %all-to-all-done.1 = f32[128,4,200]{2,1,0:T(4,128)S(1)} async-done(((f32[128,4,200]{2,1,0:T(4,128)}), f32[128,4,200]{2,1,0:T(4,128)S(1)}, u32[]{:S(2)}, u32[]{:S(2)}) %all-to-all-start.1) | async-done | bytes 409632 | tf_op jit(solution)/shard_map/all_to_all | solution.py:85
  71.6 1.6 gather_fusion.1
  74.1 7.1 %multiply_convert_fusion = (bf16[128,32,38,8]{0,1,3,2:T(8,128)(2,1)S(1)}, f32[128,32,38,8]{0,1,3,2:T(8,128)}) fusion(f32[32,1,3,3]{0,1,3,2:T(1,128)S(1)} %reshape.195, f32[128,1,40,10]{0,2,3,1:T(8,128)S(1)} %bitcast.46), kind=kOutput, calls=%fused_computation.9 | convolution fusion | flops 140705792 | bytes 7677056 | tf_op jit(solution)/shard_map/jvp()/conv_general_dilated | solution.py:19
  82.1 1.6 copy.123
  83.8 3.5 multiply_reduce_fusion.1
  88.3 2.0 fusion.30
  90.4 2.6 fusion.1
  93.1 2.2 copy-done
  95.3 23.1 %fusion.29 = f32[128,1,40,10]{0,1,3,2:T(1,128)S(1)} fusion(f32[128,32,38,8]{0,1,3,2:T(8,128)S(1)} %fusion.1, f32[32,1,3,3]{0,1,3,2:T(1,128)S(1)} %reshape.195), kind=kOutput, calls=%fused_computation.68 | convolution fusion | flops 134479872 | bytes 5186688 | tf_op jit(solution)/shard_map/transpose(jvp())/conv_general_dilated | solution.py:19
  118.7 1.9 scatter_custom_fusion.1
  120.7 26.3 %all_to_all.25 = f32[128,4,200]{2,1,0:T(4,128)S(1)} all-to-all(f32[128,4,200]{2,1,0:T(4,128)S(1)} %reshape.138), channel_id=1, replica_groups=mesh['ent'=128,'rep'=4] {'ent'}, dimensions={0} | all-to-all | bytes 819200 | tf_op jit(solution)/shard_map/all_to_all | solution.py:97
  148.7 8.4 %all-gather = s32[512,1,4]{0,2,1:T(4,128)S(1)} all-gather(s32[128,1,4]{0,2,1:T(4,128)S(1)} %copy.96), channel_id=2, replica_groups=mesh['ent'=128,'rep'=4] {'rep'}, dimensions={0}, use_global_device_ids=true | all-gather | bytes 10240 | tf_op jit(solution)/shard_map/all_gather | solution.py:98
  157.5 9.4 %convolution_reduce_fusion = f32[32,3,3]{0,2,1:T(4,128)S(1)} fusion(f32[128,32,38,8]{0,1,3,2:T(8,128)} %copy-done, f32[128,1,40,10]{0,2,3,1:T(8,128)S(1)} %bitcast.47), kind=kOutput, calls=%fused_computation.20 | convolution fusion | flops 134479872 | bytes 5186688 | tf_op jit(solution)/shard_map/transpose(jvp())/conv_general_dilated | solution.py:19
  166.9 10.1 %all-gather.3.cloned.1.call-done = f32[512,4,200]{0,2,1:T(8,128)} async-done(((f32[128,4,200]{0,2,1:T(8,128)}), f32[512,4,200]{0,2,1:T(8,128)}) %all-gather.3.cloned.1.call-update) | async-done | bytes 1638416 | tf_op jit(solution)/shard_map/all_gather | solution.py:99
  177.0 2.0 copy.116
  179.0 1.8 reshape.187
  180.8 12.1 %scatter_custom_fusion.2 = f32[512,200]{1,0:T(8,128)S(1)} fusion(s32[2048]{0:T(1024)S(1)} %bitcast.53, f32[2048,200]{1,0:T(8,128)} %reshape.187, f32[]{:T(128)} %constant.16.clone.1), kind=kCustom, calls=%fused_computation.28 | custom fusion | flops 409600 | bytes 410112 | tf_op jit(solution)/shard_map/scatter-add | solution.py:103
  193.6 257.4 %all-reduce.1 = (f32[]{:T(128)}, f32[32,9]{0,1:T(8,128)S(1)}) all-reduce(f32[]{:T(128)} %sqrt_reduce_fusion, f32[32,9]{0,1:T(8,128)S(1)} %reshape.140), channel_id=1, replica_groups=mesh['ent'=128,'rep'=4] {'ent'}, use_global_device_ids=true, to_apply=%region_9.10 | all-reduce | flops 289 | bytes 2312 | tf_op jit(solution)/shard_map/psum | solution.py:110
  452.8 7.9 %psum.23 = f32[32,9]{0,1:T(8,128)S(1)} all-reduce(f32[32,9]{0,1:T(8,128)S(1)} %get-tuple-element.11), channel_id=1, replica_groups=mesh['ent'=128,'rep'=4] {'rep'}, use_global_device_ids=true, to_apply=%region_11.12 | all-reduce | flops 288 | bytes 2304 | tf_op jit(solution)/shard_map/psum | solution.py:108
  (83 shorter events, 14.6 us)
Async XLA Ops:
  8.0 44.3 %copy-start.5 = (bf16[822,200]{0,1:T(8,128)(2,1)S(1)}, bf16[822,200]{0,1:T(8,128)(2,1)}, u32[]{:S(2)}) copy-start(bf16[822,200]{0,1:T(8,128)(2,1)} %param.10) | copy-start | bytes 986404
  8.2 44.3 %copy-start.9 = (s32[128]{0:T(128)S(1)}, s32[128]{0:T(128)}, u32[]{:S(2)}) copy-start(s32[128]{0:T(128)} %param.15) | copy-start | bytes 1540
  8.5 45.1 %copy-start.6 = (f32[32,9]{0,1:T(8,128)S(1)}, f32[32,9]{0,1:T(8,128)}, u32[]{:S(2)}) copy-start(f32[32,9]{0,1:T(8,128)} %param.11) | copy-start | bytes 3460
  9.2 62.3 %copy-start.7 = (s32[320]{0:T(512)}, s32[320]{0:T(512)S(1)}, u32[]{:S(2)}) copy-start(s32[320]{0:T(512)S(1)} %fusion.22) | copy-start | bytes 3844
  13.1 29.9 %all-to-all-start = ((s32[128,1,4]{2,1,0:T(1,128)}), s32[128,1,4]{2,1,0:T(1,128)S(1)}, u32[]{:S(2)}, u32[]{:S(2)}) async-start(s32[128,1,4]{2,1,0:T(1,128)} %bitcast.4), calls=%async_computation | async-start | bytes 131072 | tf_op jit(solution)/shard_map/all_to_all | solution.py:83
  42.9 0.6 copy-start.2
  46.1 25.3 %all-to-all-start.1 = ((f32[128,4,200]{2,1,0:T(4,128)}), f32[128,4,200]{2,1,0:T(4,128)S(1)}, u32[]{:S(2)}, u32[]{:S(2)}) async-start(f32[128,4,200]{2,1,0:T(4,128)} %reshape.144), calls=%async_computation.1 | async-start | bytes 1048576 | tf_op jit(solution)/shard_map/all_to_all | solution.py:85
  51.8 125.2 %all-gather.3.cloned.1.call-start = ((), (), s32[]{:S(2)}) async-start(), calls=%async_computation.3 | async-start | bytes 2048000 | tf_op jit(solution)/shard_map/all_gather | solution.py:99
  83.8 4.1 copy-start.4
  83.8 4.5 copy-start.1
  87.5 2.8 slice-start
  88.3 2.1 slice-start.1
  93.1 2.2 copy-start
  95.3 53.4 %copy-start.8 = (s32[512]{0:T(512)S(1)}, s32[512]{0:T(512)}, u32[]{:S(2)}) copy-start(s32[512]{0:T(512)} %param.16) | copy-start | bytes 6148
  95.3 53.4 %copy-start.3 = (s32[128,1,4]{2,1,0:T(1,128)S(1)}, s32[128,1,4]{2,1,0:T(1,128)}, u32[]{:S(2)}) copy-start(s32[128,1,4]{2,1,0:T(1,128)} %copy-done.2) | copy-start | bytes 6148
Sparse Core Ops, SparseCore 0:
  148.1 28.8 all-gather.2
